TPU v7x, 256 devices: a whole 4x4x8 slice. The times are simulated.
256 devices in a mesh: req: 16 (over z_hi, y, core), tp: 16 (over z_lo, x).
Axes of the slice: x: 4, y: 4, z: 8 (z_hi: 2, z_lo: 4; z = z_hi * 4 + z_lo), core: 2. Of those that a mesh axis runs over, the one named last changes fastest.
Arguments:
- queries: bfloat16 [64, 32, 4096], P('req'), may hold values from -128 to 128
- cache_keys: bfloat16 [64, 4096, 512], P('req', 'tp'), may hold values from -4 to 4
- cache_values: bfloat16 [64, 4096, 512], P('req', 'tp'), may hold values from -5 to 5
- tree_keys: bfloat16 [64, 32, 512], P('req', 'tp'), may hold values from -5 to 5
- tree_values: bfloat16 [64, 32, 512], P('req', 'tp'), may hold values from -5 to 5
- parents: int32 [64, 32], P('req'), may hold values from -1 to 30, as said below
- lengths: int32 [64], P('req'), may hold values from 2 to 4096
- accepted_leaf: int32 [64], P('req'), may hold values from 0 to 31
- residual: bfloat16 [64, 32, 8192], P('req', None, 'tp'), may hold values from -12 to 12
- norm_gain: float32 [8192], replicated, may hold values from 0.5 to 4
- out_weight: bfloat16 [4096, 8192], P('tp'), may hold values from -0.09375 to 0.09375
- prev_feature: bfloat16 [64, 8192], P('req'), may hold values from -5 to 5
- draft_weight: bfloat16 [8192, 8192], P('req', 'tp'), may hold values from -0.0625 to 0.0625
- first_moment: float32 [8192, 8192], P('req', 'tp'), may hold values from -5 to 5
- second_moment: float32 [8192, 8192], P('req', 'tp'), may hold values from 0.25 to 4
Outputs:
- features: bfloat16 [64, 32, 8192], P('req', None, 'tp')
- new_weight: bfloat16 [8192, 8192], P('req', 'tp')
- new_first: float32 [8192, 8192], P('req', 'tp')
- new_second: float32 [8192, 8192], P('req', 'tp')
- draft_loss: float32 [], replicated
Inputs may be any that keep to these rules, and one draw needn't show every extreme that they name: parents[r, 0] = -1; for i of 1 or more, parents[r, i] lies in 0 to i - 1; node 31 is a child of node 30.
All inputs are finite; a program needn't handle non-finite values.
Results may differ from a plain program's by a relative error of at most 0.014.
Values may be sent and summed in bfloat16 or wider, within the bound.
No kernel may reach another device: no remote copies, remote signals or barrier semaphores. Data moves between devices by JAX's collectives and lax.ppermute only.
A program may use at most 128 MiB of HBM per device.

v0:
```python
import math
import jax
import jax.numpy as jnp
from jax import lax
from jax.sharding import PartitionSpec as P

HEADS = 32
KV_HEADS = 4
HEAD = 128
NODES = 32
CACHE = 4096
NEG_FILL = -1e30
NORM_EPSILON = 1e-06
BETA_ONE = 0.9
BETA_TWO = 0.95
CORRECT_ONE = 1.0 - 0.9**10
CORRECT_TWO = 1.0 - 0.95**10
LEARN_RATE = 0.001


def closure(parents):
    node_count = parents.shape[-1]
    onehot = (parents[:, :, None] == jnp.arange(node_count, dtype=jnp.int32)[None, None, :]).astype(
        jnp.float32
    )
    reach_map = jnp.eye(node_count, dtype=jnp.float32)[None] + onehot
    for repeat in range(node_count.bit_length()):
        reach_map = jnp.minimum(
            jnp.einsum("rij,rjk->rik", reach_map, reach_map, precision=lax.Precision.HIGHEST), 1.0
        )
    return reach_map


def body(
    queries,
    cache_keys,
    cache_values,
    tree_keys,
    tree_values,
    parents,
    lengths,
    accepted_leaf,
    residual,
    norm_gain,
    out_weight,
    prev_feature,
    draft_weight,
    first_moment,
    second_moment,
):
    full_residual = lax.all_gather(residual, "tp", axis=2, tiled=True)
    requests = queries.shape[0]
    row_count = requests * NODES
    groups = HEADS // KV_HEADS
    score_scale = 1.0 / math.sqrt(HEAD)
    tp_rank = lax.axis_index("tp")
    cache_span = cache_keys.shape[1]
    tree_span = tree_keys.shape[1]
    reach_map = closure(parents)
    query_view = queries.reshape(requests, NODES, KV_HEADS, groups, HEAD)
    cache_view = cache_keys.reshape(requests, cache_span, KV_HEADS, HEAD)
    tree_view = tree_keys.reshape(requests, tree_span, KV_HEADS, HEAD)
    cache_scores = (
        jnp.einsum("rnkgd,rckd->rkgnc", query_view, cache_view, preferred_element_type=jnp.float32)
        * score_scale
    )
    tree_scores = (
        jnp.einsum("rnkgd,rjkd->rkgnj", query_view, tree_view, preferred_element_type=jnp.float32)
        * score_scale
    )
    positions = tp_rank * cache_span + jnp.arange(cache_span, dtype=jnp.int32)
    cache_live = (positions[None, :] < lengths[:, None])[:, None, None, None, :]
    visible = lax.dynamic_slice_in_dim(reach_map, tp_rank * tree_span, tree_span, 2)
    tree_live = (visible > 0.5)[:, None, None, :, :]
    cache_scores = jnp.where(cache_live, cache_scores, NEG_FILL)
    tree_scores = jnp.where(tree_live, tree_scores, NEG_FILL)
    local_top = jnp.maximum(jnp.max(cache_scores, axis=-1), jnp.max(tree_scores, axis=-1))
    row_top = lax.pmax(local_top, "tp")
    cache_probs = jnp.where(cache_live, jnp.exp(cache_scores - row_top[..., None]), 0.0).astype(
        jnp.bfloat16
    )
    tree_probs = jnp.where(tree_live, jnp.exp(tree_scores - row_top[..., None]), 0.0).astype(
        jnp.bfloat16
    )
    totals = jnp.sum(cache_probs, axis=-1, dtype=jnp.float32) + jnp.sum(
        tree_probs, axis=-1, dtype=jnp.float32
    )
    value_view = cache_values.reshape(requests, cache_span, KV_HEADS, HEAD)
    tree_value_view = tree_values.reshape(requests, tree_span, KV_HEADS, HEAD)
    weighted = jnp.einsum(
        "rkgnc,rckd->rnkgd", cache_probs, value_view, preferred_element_type=jnp.float32
    )
    weighted = weighted + jnp.einsum(
        "rkgnj,rjkd->rnkgd", tree_probs, tree_value_view, preferred_element_type=jnp.float32
    )
    weighted = weighted.reshape(row_count, HEADS * HEAD)
    totals = jnp.transpose(totals, (0, 3, 1, 2)).reshape(row_count, HEADS)
    head_sums, head_totals = (
        lax.psum_scatter(weighted, "tp", scatter_dimension=1, tiled=True),
        lax.psum_scatter(totals, "tp", scatter_dimension=1, tiled=True),
    )
    own_heads = head_totals.shape[1]
    attended = (head_sums.reshape(row_count, own_heads, HEAD) / head_totals[:, :, None]).astype(
        jnp.bfloat16
    )
    partial_value = jnp.dot(
        attended.reshape(row_count, own_heads * HEAD),
        out_weight,
        preferred_element_type=jnp.float32,
    )
    partial_value = lax.optimization_barrier(partial_value.astype(jnp.bfloat16)).astype(jnp.float32)
    model_width = partial_value.shape[1]
    block_width = model_width // lax.axis_size("tp")
    summed = lax.psum(partial_value.astype(jnp.bfloat16), "tp").astype(jnp.float32)
    mixed = full_residual.reshape(row_count, model_width).astype(jnp.float32) + summed
    mean_sq = jnp.mean(mixed * mixed, axis=1, keepdims=True)
    features = (mixed * lax.rsqrt(mean_sq + NORM_EPSILON) * norm_gain[None, :]).astype(jnp.bfloat16)
    own_block = lax.dynamic_slice_in_dim(features, tp_rank * block_width, block_width, 1)
    feature_table = jnp.concatenate(
        [prev_feature[:, None, :], features.reshape(requests, NODES, model_width)], axis=1
    )
    inputs = jnp.take_along_axis(feature_table, (parents + 1)[:, :, None], axis=1).reshape(
        row_count, model_width
    )
    leaf_hot = (accepted_leaf[:, None] == jnp.arange(NODES, dtype=jnp.int32)[None, :]).astype(
        jnp.float32
    )
    accepted = jnp.einsum("rn,rnj->rj", leaf_hot, reach_map, precision=lax.Precision.HIGHEST)
    fill_share = 0.5 + lengths.astype(jnp.float32) / CACHE
    weights = ((1.0 + 3.0 * accepted) * fill_share[:, None]).reshape(row_count, 1)
    columns = inputs
    predicted = jnp.dot(
        columns,
        lax.all_gather(draft_weight, "req", axis=0, tiled=True),
        preferred_element_type=jnp.float32,
    )
    pred_error = predicted - own_block.astype(jnp.float32)
    scaled_err = (weights * pred_error).astype(jnp.bfloat16)
    columns = inputs
    gradient = lax.psum_scatter(
        lax.dot_general(
            columns, scaled_err, (((0,), (0,)), ((), ())), preferred_element_type=jnp.float32
        ),
        "req",
        scatter_dimension=0,
        tiled=True,
    )
    square_total, error_total = lax.psum(
        (jnp.sum(gradient * gradient), jnp.sum(weights * pred_error * pred_error)), ("req", "tp")
    )
    draft_loss = 0.5 * error_total / (row_count * lax.axis_size("req") * model_width)
    grad_norm = jnp.sqrt(square_total) + 1e-06
    clip_factor = jnp.minimum(1.0, model_width / grad_norm)
    clipped = gradient * clip_factor
    new_first = BETA_ONE * first_moment + (1.0 - BETA_ONE) * clipped
    new_second = BETA_TWO * second_moment + (1.0 - BETA_TWO) * clipped * clipped
    direction = new_first / CORRECT_ONE / (jnp.sqrt(new_second / CORRECT_TWO) + 1e-08)
    new_weight = (draft_weight.astype(jnp.float32) - LEARN_RATE * direction).astype(jnp.bfloat16)
    return (
        own_block.reshape(requests, NODES, block_width),
        new_weight,
        new_first,
        new_second,
        draft_loss,
    )


def solution(mesh):
    placed = (
        P("req", None, None),
        P("req", "tp", None),
        P("req", "tp", None),
        P("req", "tp", None),
        P("req", "tp", None),
        P("req", None),
        P("req"),
        P("req"),
        P("req", None, "tp"),
        P(),
        P("tp", None),
        P("req", None),
        P("req", "tp"),
        P("req", "tp"),
        P("req", "tp"),
    )
    return jax.shard_map(
        body,
        mesh=mesh,
        in_specs=placed,
        out_specs=(P("req", None, "tp"), P("req", "tp"), P("req", "tp"), P("req", "tp"), P()),
        check_vma=False,
    )
```

profile of v0, /device:TPU:1, one launch (start us, length us, event | category | flops | bytes accessed | tf_op | source)
XLA Modules:
  0.0 868.4 jit_solution(2874297902461404456)
XLA Ops:
  10.4 1.4 copy.89
  13.3 1.5 fusion.38
  14.8 4.1 bitcast_reduce_fusion
  19.0 67.8 %pmax.7 = f32[4,4,8,32]{3,2,1,0:T(8,128)S(1)} all-reduce(f32[4,4,8,32]{3,2,1,0:T(8,128)S(1)} %max.5), channel_id=1, replica_groups=mesh['req'=16,'tp'=16] {'tp'}, use_global_device_ids=true, to_apply=%region_2.3 | all-reduce | flops 4096 | bytes 32768 | tf_op jit(solution)/shard_map/pmax | solution.py:78
  87.0 3.0 fusion.6
  90.5 1.2 copy.74
  91.7 1.5 reshape.112
  94.1 3.1 convert_reduce_fusion
  98.6 61.0 %all-reduce = f32[128,32]{0,1:T(8,128)S(1)} all-reduce(f32[128,32]{0,1:T(8,128)S(1)} %reshape.113), channel_id=3, replica_groups=mesh['req'=16,'tp'=16] {'tp'}, use_global_device_ids=true, to_apply=%region_6.7.clone | all-reduce | flops 4096 | bytes 32768
  159.7 23.9 %reduce-scatter.3.cloned.1.call-done = f32[128,256]{1,0:T(8,128)} async-done(((f32[128,4096]{1,0:T(8,128)}), f32[128,256]{1,0:T(8,128)}) %reduce-scatter.3.cloned.1.call-update) | async-done | bytes 131088 | tf_op jit(solution)/shard_map/reduce_scatter | solution.py:99
  183.9 4.3 convolution_convert_fusion
  189.7 75.2 %all-gather.3.cloned.1.call-done = bf16[4,32,8192]{2,1,0:T(8,128)(2,1)} async-done(((bf16[4,32,512]{2,1,0:T(8,128)(2,1)}), bf16[4,32,8192]{2,1,0:T(8,128)(2,1)}) %all-gather.3.cloned.1.call-update) | async-done | bytes 2097168 | tf_op jit(solution)/shard_map/all_gather | solution.py:51
  264.8 168.2 %all-reduce.4.cloned.1.call-done = bf16[128,8192]{1,0:T(8,128)(2,1)} async-done(((bf16[128,8192]{1,0:T(8,128)(2,1)}), bf16[128,8192]{1,0:T(8,128)(2,1)}) %all-reduce.4.cloned.1.call-update) | async-done | bytes 2097168 | tf_op jit(solution)/shard_map/psum | solution.py:114
  433.0 3.1 multiply_reduce_fusion
  437.2 1.6 copy.77
  438.9 1.4 pad_maximum_fusion
  440.3 8.3 gather_fusion
  449.5 103.7 %all-gather.5.cloned.1.call-done = bf16[8192,512]{1,0:T(8,128)(2,1)} async-done(((bf16[512,512]{1,0:T(8,128)(2,1)}), bf16[8192,512]{1,0:T(8,128)(2,1)}) %all-gather.5.cloned.1.call-update) | async-done | bytes 8388624 | tf_op jit(solution)/shard_map/all_gather | solution.py:134
  553.2 6.2 fusion.13
  559.4 8.2 fusion.12
  567.6 210.0 %reduce-scatter.5.cloned.1.call-done = f32[512,512]{1,0:T(8,128)} async-done(((f32[8192,512]{1,0:T(8,128)}), f32[512,512]{1,0:T(8,128)}) %reduce-scatter.5.cloned.1.call-update) | async-done | bytes 1048592 | tf_op jit(solution)/shard_map/reduce_scatter | solution.py:140
  777.6 2.1 multiply_reduce_fusion.1
  779.7 76.2 %all-reduce.1 = (f32[]{:T(128)}, f32[]{:T(128)}) all-reduce(f32[]{:T(128)} %multiply_reduce_fusion.1, f32[]{:T(128)} %get-tuple-element.16), channel_id=1, replica_groups=mesh['req'=16,'tp'=16] {'req','tp'}, use_global_device_ids=true, to_apply=%region_11.12 | all-reduce | flops 2 | bytes 16 | tf_op jit(solution)/shard_map/psum | solution.py:148
  857.3 3.4 subtract_convert_fusion
  (89 shorter events, 10.6 us)
Async XLA Ops:
  7.2 82.8 %copy-start = (bf16[4,2,512]{2,1,0:T(2,128)(2,1)S(1)}, bf16[4,2,512]{2,1,0:T(2,128)(2,1)}, u32[]{:S(2)}) copy-start(bf16[4,2,512]{2,1,0:T(2,128)(2,1)} %param.19) | copy-start | bytes 24580
  7.2 4.7 copy-start.9
  7.2 5.8 copy-start.10
  7.2 6.0 copy-start.15
  7.2 6.1 copy-start.16
  7.2 176.4 %reduce-scatter.3.cloned.1.call-start = ((), (), s32[]{:S(2)}) async-start(), calls=%async_computation.3 | async-start | bytes 2228224 | tf_op jit(solution)/shard_map/reduce_scatter | solution.py:99
  93.2 4.2 copy-start.18
  93.3 171.5 %all-gather.3.cloned.1.call-start = ((), (), s32[]{:S(2)}) async-start(), calls=%async_computation.2 | async-start | bytes 2228224 | tf_op jit(solution)/shard_map/all_gather | solution.py:51
  94.0 338.9 %all-reduce.4.cloned.1.call-start = ((), (), s32[]{:S(2)}) async-start(), calls=%async_computation.4 | async-start | bytes 4194304 | tf_op jit(solution)/shard_map/psum | solution.py:114
  183.9 5.2 copy-start.14
  183.9 5.4 copy-start.17
  188.2 247.9 %copy-start.13 = (f32[8192]{0:T(1024)S(1)}, f32[8192]{0:T(1024)}, u32[]{:S(2)}) copy-start(f32[8192]{0:T(1024)} %param.24) | copy-start | bytes 98308
  188.2 365.0 %all-gather.5.cloned.1.call-start = ((), (), s32[]{:S(2)}) async-start(), calls=%async_computation.5 | async-start | bytes 8912896 | tf_op jit(solution)/shard_map/all_gather | solution.py:134
  188.8 588.8 %reduce-scatter.5.cloned.1.call-start = ((), (), s32[]{:S(2)}) async-start(), calls=%async_computation.6 | async-start | bytes 17825792 | tf_op jit(solution)/shard_map/reduce_scatter | solution.py:140
  264.8 171.3 %copy-start.4 = (bf16[4,32,8192]{2,1,0:T(8,128)(2,1)S(1)}, bf16[4,32,8192]{2,1,0:T(8,128)(2,1)}, u32[]{:S(2)}) copy-start(bf16[4,32,8192]{2,1,0:T(8,128)(2,1)} %all-gather.3.cloned.1.call-done) | copy-start | bytes 6291460
  433.0 3.2 copy-start.5
  436.1 2.7 copy-start.12
  437.2 1.6 copy-start.3
  449.5 109.9 %copy-start.11 = (bf16[128,512]{1,0:T(8,128)(2,1)}, bf16[128,512]{1,0:T(8,128)(2,1)S(1)}, u32[]{:S(2)}) copy-start(bf16[128,512]{1,0:T(8,128)(2,1)S(1)} %constant_dynamic-slice_fusion.1) | copy-start | bytes 393220
  449.5 109.9 %copy-start.2 = (bf16[128,8192]{1,0:T(8,128)(2,1)S(1)}, bf16[128,8192]{1,0:T(8,128)(2,1)}, u32[]{:S(2)}) copy-start(bf16[128,8192]{1,0:T(8,128)(2,1)} %gather_fusion) | copy-start | bytes 6291460
  567.6 289.7 %copy-start.6 = (bf16[512,512]{1,0:T(8,128)(2,1)S(1)}, bf16[512,512]{1,0:T(8,128)(2,1)}, u32[]{:S(2)}) copy-start(bf16[512,512]{1,0:T(8,128)(2,1)} %param.27) | copy-start | bytes 1572868
  567.6 289.7 %copy-start.7 = (f32[512,512]{1,0:T(8,128)S(1)}, f32[512,512]{1,0:T(8,128)}, u32[]{:S(2)}) copy-start(f32[512,512]{1,0:T(8,128)} %param.28) | copy-start | bytes 3145732
  567.6 289.7 %copy-start.8 = (f32[512,512]{1,0:T(8,128)S(1)}, f32[512,512]{1,0:T(8,128)}, u32[]{:S(2)}) copy-start(f32[512,512]{1,0:T(8,128)} %param.29) | copy-start | bytes 3145732
  567.6 293.1 %copy-start.1 = (bf16[4,2,512]{2,1,0:T(2,128)(2,1)S(1)}, bf16[4,2,512]{2,1,0:T(2,128)(2,1)}, u32[]{:S(2)}) copy-start(bf16[4,2,512]{2,1,0:T(2,128)(2,1)} %param.19) | copy-start | bytes 24580
Sparse Core Ops, SparseCore 0:
  93.4 90.2 reduce-scatter.2
  185.5 79.3 all-gather.2
  267.5 165.4 all-reduce.3
  435.6 117.5 all-gather.4
  567.7 209.8 reduce-scatter.4
where the time goes:
time: 869 us; the launch traced here: 868 us
  waiting for transfers between devices  582 us (67%)
  blocking collectives  205 us (24%)
  matrix products  30.4 us (3%)
  local copies, waits for them, and re-layouts  18.2 us (2%)
  between operations  17.4 us (2%)
  other arithmetic  14.8 us (2%)
    reduce_scatter x1, waiting for transfers between devices, body(): lax.psum_scatter(lax.dot_general(columns, scaled_err, (((0,), (0,)), ((),...  210 us
    psum x1, waiting for transfers between devices, body(): lax.psum(partial_value.astype(jnp.bfloat16), 'tp').astype(jnp.float32)  168 us
    all_gather x1, waiting for transfers between devices, body(): lax.all_gather(draft_weight, 'req', axis=0, tiled=True)  104 us
    psum x1, blocking collectives, body(): lax.psum((jnp.sum(gradient * gradient), jnp.sum(weights * pred_error * pr...  76.2 us
    all_gather x1, waiting for transfers between devices, body(): full_residual = lax.all_gather(residual, 'tp', axis=2, tiled=True)  75.2 us
    pmax x1, blocking collectives, body(): row_top = lax.pmax(local_top, 'tp')  67.8 us
    unnamed x1, blocking collectives  61 us
    reduce_scatter x1, waiting for transfers between devices, body(): lax.psum_scatter(weighted, 'tp', scatter_dimension=1, tiled=True)  23.9 us
  transfers between devices with their start and end apart: 5, of which 5 were waited for; matrix products, arithmetic and copies ran while one was open for 3% of the time, Pallas kernels for 0%

commit v1 on v0

--- a/solution.py
+++ b/solution.py
@@ -16,6 +16,11 @@
 CORRECT_ONE = 1.0 - 0.9**10
 CORRECT_TWO = 1.0 - 0.95**10
 LEARN_RATE = 0.001
+
+
+def exchange_gather(x, mesh_axis, along):
+    sent = jnp.stack([x] * lax.axis_size(mesh_axis))
+    return jnp.concatenate(lax.all_to_all(sent, mesh_axis, 0, 0), axis=along)
 
 
 def closure(parents):
@@ -48,7 +53,7 @@
     first_moment,
     second_moment,
 ):
-    full_residual = lax.all_gather(residual, "tp", axis=2, tiled=True)
+    full_residual = exchange_gather(residual, "tp", 2)
     requests = queries.shape[0]
     row_count = requests * NODES
     groups = HEADS // KV_HEADS

time: 869 us -> 764 us (0.88)
  waiting for transfers between devices: 582 us -> 462 us
  local copies, waits for them, and re-layouts: 18.2 us -> 28.1 us
    all_gather x1, waiting for transfers between devices: 104 us -> 0.03 us  [body(): lax.all_gather(draft_weight, 'req', axis=0, tiled=True)]
    all_gather x1 -> x0, waiting for transfers between devices: 75.2 us -> none  [body(): full_residual = lax.all_gather(residual, 'tp', axis=2, tiled=True)]
    all_to_all x0 -> x1, waiting for transfers between devices: none -> 51.8 us  [exchange_gather(): return jnp.concatenate(lax.all_to_all(sent, mesh_axis, 0, 0), axis=along)]
    reduce_scatter x1, waiting for transfers between devices: 210 us -> 224 us  [body(): lax.psum_scatter(lax.dot_general(columns, scaled_err, (((0,), (0,)), ((),...]
  transfers between devices with their start and end apart: 5 -> 5, of which waited for: 5 -> 4; matrix products, arithmetic and copies ran while one was open for 3% -> 4% of each run, Pallas kernels for 0% -> 0%
where the time goes in v1:
time: 764 us; the launch traced here: 763 us
  waiting for transfers between devices  462 us (60%)
  blocking collectives  205 us (27%)
  matrix products  29 us (4%)
  local copies, waits for them, and re-layouts  28.1 us (4%)
  between operations  19.1 us (3%)
  other arithmetic  15.5 us (2%)
    reduce_scatter x1, waiting for transfers between devices, body(): lax.psum_scatter(lax.dot_general(columns, scaled_err, (((0,), (0,)), ((),...  224 us
    psum x1, waiting for transfers between devices, body(): lax.psum(partial_value.astype(jnp.bfloat16), 'tp').astype(jnp.float32)  161 us
    psum x1, blocking collectives, body(): lax.psum((jnp.sum(gradient * gradient), jnp.sum(weights * pred_error * pr...  76.3 us
    pmax x1, blocking collectives, body(): row_top = lax.pmax(local_top, 'tp')  67.8 us
    unnamed x1, blocking collectives  61.4 us
    all_to_all x1, waiting for transfers between devices, exchange_gather(): return jnp.concatenate(lax.all_to_all(sent, mesh_axis, 0, 0), axis=along)  51.8 us
    reduce_scatter x1, waiting for transfers between devices, body(): lax.psum_scatter(weighted, 'tp', scatter_dimension=1, tiled=True)  24.4 us
  transfers between devices with their start and end apart: 5, of which 4 were waited for; matrix products, arithmetic and copies ran while one was open for 4% of the time, Pallas kernels for 0%

profile of v1, /device:TPU:1, one launch (start us, length us, event | category | flops | bytes accessed | tf_op | source)
XLA Modules:
  0.0 763.3 jit_solution(13286843295787321085)
XLA Ops:
  13.0 1.5 fusion.38
  14.5 2.9 bitcast_reduce_fusion
  17.4 67.8 %pmax.7 = f32[4,4,8,32]{3,2,1,0:T(8,128)S(1)} all-reduce(f32[4,4,8,32]{3,2,1,0:T(8,128)S(1)} %max.5), channel_id=1, replica_groups=mesh['req'=16,'tp'=16] {'tp'}, use_global_device_ids=true, to_apply=%region_2.3 | all-reduce | flops 4096 | bytes 32768 | tf_op jit(solution)/shard_map/pmax | solution.py:83
  85.7 2.9 fusion.6
  90.4 1.5 reshape.114
  92.0 3.1 convert_reduce_fusion
  96.6 61.4 %all-reduce = f32[128,32]{0,1:T(8,128)S(1)} all-reduce(f32[128,32]{0,1:T(8,128)S(1)} %reshape.115), channel_id=3, replica_groups=mesh['req'=16,'tp'=16] {'tp'}, use_global_device_ids=true, to_apply=%region_6.7.clone | all-reduce | flops 4096 | bytes 32768
  158.1 24.4 %reduce-scatter.3.cloned.1.call-done = f32[128,256]{1,0:T(8,128)} async-done(((f32[128,4096]{1,0:T(8,128)}), f32[128,256]{1,0:T(8,128)}) %reduce-scatter.3.cloned.1.call-update) | async-done | bytes 131088 | tf_op jit(solution)/shard_map/reduce_scatter | solution.py:104
  182.8 4.3 convolution_convert_fusion
  187.7 1.6 stack.2
  189.3 3.7 all-to-all-start
  193.9 51.8 %all-to-all-done = bf16[16,4,32,512]{3,2,1,0:T(8,128)(2,1)S(1)} async-done(((bf16[16,4,32,512]{3,2,1,0:T(8,128)(2,1)}), bf16[16,4,32,512]{3,2,1,0:T(8,128)(2,1)S(1)}, u32[]{:S(2)}, u32[]{:S(2)}) %all-to-all-start) | async-done | bytes 2097184 | tf_op jit(solution)/shard_map/all_to_all | solution.py:23
  246.3 2.4 copy.52
  248.8 5.4 copy.91
  254.2 160.8 %all-reduce.4.cloned.1.call-done = bf16[128,8192]{1,0:T(8,128)(2,1)} async-done(((bf16[128,8192]{1,0:T(8,128)(2,1)}), bf16[128,8192]{1,0:T(8,128)(2,1)}) %all-reduce.4.cloned.1.call-update) | async-done | bytes 2097168 | tf_op jit(solution)/shard_map/psum | solution.py:119
  415.0 3.6 multiply_reduce_fusion
  420.5 1.6 copy.79
  423.5 8.5 %gather_fusion = bf16[128,8192]{1,0:T(8,128)(2,1)} fusion(bf16[4,33,8192]{2,0,1:T(4,128)(2,1)S(1)} %pad_maximum_fusion, s32[128]{0:T(128)S(1)} %reshape.119), kind=kCustom, calls=%fused_computation | custom fusion | bytes 4195328 | tf_op jit(solution)/shard_map/jit(take_along_axis)/gather | solution.py:127
  433.0 6.1 fusion.13
  439.1 8.2 %fusion.12 = f32[8192,512]{1,0:T(8,128)} fusion(bf16[128,8192]{1,0:T(8,128)(2,1)S(1)} %copy-done.3, pred[128]{0:T(512)(128)(4,1)S(1)} %broadcast_in_dim.74, f32[128,512]{1,0:T(8,128)S(1)} %get-tuple-element.17, f32[128]{0:T(128)S(1)} %mul.137), kind=kOutput, calls=%fused_computation.36 | convolution fusion | flops 1074921472 | bytes 19137152 | tf_op jit(solution)/shard_map/dot_general | solution.py:146
  447.3 224.3 %reduce-scatter.5.cloned.1.call-done = f32[512,512]{1,0:T(8,128)} async-done(((f32[8192,512]{1,0:T(8,128)}), f32[512,512]{1,0:T(8,128)}) %reduce-scatter.5.cloned.1.call-update) | async-done | bytes 1048592 | tf_op jit(solution)/shard_map/reduce_scatter | solution.py:145
  671.6 2.1 multiply_reduce_fusion.1
  673.7 76.3 %all-reduce.1 = (f32[]{:T(128)}, f32[]{:T(128)}) all-reduce(f32[]{:T(128)} %multiply_reduce_fusion.1, f32[]{:T(128)} %get-tuple-element.16), channel_id=1, replica_groups=mesh['req'=16,'tp'=16] {'req','tp'}, use_global_device_ids=true, to_apply=%region_11.12 | all-reduce | flops 2 | bytes 16 | tf_op jit(solution)/shard_map/psum | solution.py:153
  751.3 3.4 subtract_convert_fusion
  (94 shorter events, 14.4 us)
Async XLA Ops:
  8.0 80.7 %copy-start = (bf16[4,2,512]{2,1,0:T(2,128)(2,1)S(1)}, bf16[4,2,512]{2,1,0:T(2,128)(2,1)}, u32[]{:S(2)}) copy-start(bf16[4,2,512]{2,1,0:T(2,128)(2,1)} %param.19) | copy-start | bytes 24580
  8.0 4.6 copy-start.9
  8.0 4.9 copy-start.16
  8.0 5.0 copy-start.17
  8.0 174.5 %reduce-scatter.3.cloned.1.call-start = ((), (), s32[]{:S(2)}) async-start(), calls=%async_computation.3 | async-start | bytes 2228224 | tf_op jit(solution)/shard_map/reduce_scatter | solution.py:104
  13.0 72.2 %copy-start.10 = (bf16[4,256,512]{2,1,0:T(8,128)(2,1)S(1)}, bf16[4,256,512]{2,1,0:T(8,128)(2,1)}, u32[]{:S(2)}) copy-start(bf16[4,256,512]{2,1,0:T(8,128)(2,1)} %param.17) | copy-start | bytes 3145732
  92.0 3.4 copy-start.19
  92.0 323.0 %all-reduce.4.cloned.1.call-start = ((), (), s32[]{:S(2)}) async-start(), calls=%async_computation.4 | async-start | bytes 4194304 | tf_op jit(solution)/shard_map/psum | solution.py:119
  182.7 5.0 copy-start.11
  187.1 6.2 copy-start.15
  187.1 6.3 copy-start.18
  187.1 245.8 %all-gather.2.cloned.1.call-start = ((), (), s32[]{:S(2)}) async-start(), calls=%async_computation.5 | async-start | bytes 8912896 | tf_op jit(solution)/shard_map/all_gather | solution.py:139
  189.3 56.4 %all-to-all-start = ((bf16[16,4,32,512]{3,2,1,0:T(8,128)(2,1)}), bf16[16,4,32,512]{3,2,1,0:T(8,128)(2,1)S(1)}, u32[]{:S(2)}, u32[]{:S(2)}) async-start(bf16[16,4,32,512]{3,2,1,0:T(8,128)(2,1)} %stack.2), calls=%async_computation | async-start | bytes 4194304 | tf_op jit(solution)/shard_map/all_to_all | solution.py:23
  193.1 478.5 %reduce-scatter.5.cloned.1.call-start = ((), (), s32[]{:S(2)}) async-start(), calls=%async_computation.6 | async-start | bytes 17825792 | tf_op jit(solution)/shard_map/reduce_scatter | solution.py:145
  248.8 169.9 %copy-start.14 = (f32[8192]{0:T(1024)S(1)}, f32[8192]{0:T(1024)}, u32[]{:S(2)}) copy-start(f32[8192]{0:T(1024)} %param.24) | copy-start | bytes 98308
  415.0 4.1 copy-start.2
  415.0 4.7 copy-start.5
  420.4 1.7 copy-start.4
  432.9 6.2 copy-start.12
  432.9 6.2 copy-start.3
  447.3 304.1 %copy-start.6 = (bf16[512,512]{1,0:T(8,128)(2,1)S(1)}, bf16[512,512]{1,0:T(8,128)(2,1)}, u32[]{:S(2)}) copy-start(bf16[512,512]{1,0:T(8,128)(2,1)} %param.27) | copy-start | bytes 1572868
  447.3 304.1 %copy-start.7 = (f32[512,512]{1,0:T(8,128)S(1)}, f32[512,512]{1,0:T(8,128)}, u32[]{:S(2)}) copy-start(f32[512,512]{1,0:T(8,128)} %param.28) | copy-start | bytes 3145732
  447.3 304.1 %copy-start.8 = (f32[512,512]{1,0:T(8,128)S(1)}, f32[512,512]{1,0:T(8,128)}, u32[]{:S(2)}) copy-start(f32[512,512]{1,0:T(8,128)} %param.29) | copy-start | bytes 3145732
  447.3 307.4 %copy-start.1 = (bf16[4,2,512]{2,1,0:T(2,128)(2,1)S(1)}, bf16[4,2,512]{2,1,0:T(2,128)(2,1)}, u32[]{:S(2)}) copy-start(bf16[4,2,512]{2,1,0:T(2,128)(2,1)} %param.19) | copy-start | bytes 24580
  (1 other events, 1.7 us)
Sparse Core Ops, SparseCore 0:
  92.1 90.3 reduce-scatter.2
  187.2 227.7 all-reduce.3
Sparse Core Ops, SparseCore 1:
  190.3 98.2 all-gather.1
  447.4 224.1 reduce-scatter.4
